TPU v7x, 256 devices: a whole 4x4x8 slice. The times are simulated.
256 devices in a mesh: dp: 64 (over y, z, core), mp: 4 (over x).
Axes of the slice: x: 4, y: 4, z: 8, core: 2. Of those that a mesh axis runs over, the one named last changes fastest.
Arguments:
- features: bfloat16 [262144, 1024], P('dp', 'mp'), may hold values from -6 to 6
- history: bfloat16 [131072, 1024], P('dp', 'mp'), may hold values from -6 to 6
- adj_values: bfloat16 [2048, 8, 128, 128], P('dp'), may hold values from -0.1875 to 0.1875
- adj_sources: int32 [2048, 8], P('dp'), may hold values from 0 to 191, as said below
- pull_list: int32 [64, 64, 2], P('dp'), may hold values from 0 to 15
- pull_count: int32 [64, 64], P('dp'), may hold values from 0 to 2, as said below
- partner_mask: int32 [1], replicated, may hold values from 1 to 63
- weight: bfloat16 [1024, 1024], P('mp'), may hold values from -0.1875 to 0.1875
- bias: float32 [1024], P('mp'), may hold values from -3 to 3
Outputs:
- layer_out: bfloat16 [262144, 1024], P('dp', 'mp')
Inputs may be any that keep to these rules, and one draw needn't show every extreme that they name: The partner of cluster c is cluster c XOR partner_mask[0]. Slots s >= pull_count[c, o] of pull_list[c, o] are not live; in every draw some owner has all 2 slots live for every cluster. `adj_sources`: indexes sources: own blocks, then partner blocks, then pulled slots; tile 0 of every target block names an own block and tile 1 a partner block. `pull_list`: local block numbers within an owner's history.
All inputs are finite; a program needn't handle non-finite values.
Results may differ from a plain program's by a relative error of at most 0.0045.
Values may be sent and summed in bfloat16 or wider, within the bound.
A program may use at most 128 MiB of HBM per device.

v0:
```python
import jax
import jax.numpy as jnp
from jax import lax
from jax.sharding import PartitionSpec as P


def from_partner(value, axis, distance):
    mask = 2**distance
    pairs = [(source, source ^ mask) for source in range(lax.axis_size(axis))]
    return lax.ppermute(value, axis, pairs)


def per_device(
    features, history, adj_values, adj_sources, pull_list, pull_count, partner_mask, weight, bias
):
    row_count, width = features.shape
    block_rows = 128
    row_blocks = row_count // block_rows
    dev_count = lax.axis_size("dp")
    partner_rows = features
    for bit_number in range(dev_count.bit_length() - 1):
        received = from_partner(partner_rows, "dp", bit_number)
        chosen = partner_mask[0] // (1 << bit_number) % 2 == 1
        partner_rows = jnp.where(chosen, received, partner_rows)
    hist_blocks = history.reshape(-1, block_rows, width)
    pulled = lax.all_to_all(
        hist_blocks[lax.all_to_all(pull_list[0], "dp", split_axis=0, concat_axis=0, tiled=True)],
        "dp",
        split_axis=0,
        concat_axis=0,
        tiled=True,
    )
    slot_total = pulled.shape[1]
    live_slots = jnp.arange(slot_total, dtype=jnp.int32)[None, :] < pull_count[0][:, None]
    pulled = jnp.where(live_slots[:, :, None, None], pulled, jnp.zeros((), pulled.dtype))
    sources = jnp.concatenate(
        [
            features.reshape(row_blocks, block_rows, width),
            partner_rows.reshape(row_blocks, block_rows, width),
            pulled.reshape(-1, block_rows, width),
        ],
        axis=0,
    )
    gathered = sources[adj_sources]
    agg = jnp.einsum("tkij,tkjd->tid", adj_values, gathered, preferred_element_type=jnp.float32)
    agg = agg.reshape(row_count, width).astype(jnp.bfloat16)
    term = jnp.dot(agg, weight, preferred_element_type=jnp.float32)
    mixed = lax.psum_scatter(term, "mp", scatter_dimension=1, tiled=True)
    return jnp.maximum(mixed + bias, 0.0).astype(jnp.bfloat16)


def solution(mesh):
    in_specs = (
        P("dp", "mp"),
        P("dp", "mp"),
        P("dp", None, None, None),
        P("dp", None),
        P("dp", None, None),
        P("dp", None),
        P(),
        P("mp", None),
        P("mp"),
    )
    out_specs = P("dp", "mp")
    return jax.shard_map(
        per_device, mesh=mesh, in_specs=in_specs, out_specs=out_specs, check_vma=False
    )
```

profile of v0, /device:TPU:1, one launch (start us, length us, event | category | flops | bytes accessed | tf_op | source)
XLA Modules:
  0.0 784.0 jit_solution(634889544934004723)
XLA Ops:
  6.5 3.2 collective-permute-start
  11.2 10.0 %all-to-all-start = ((s32[64,1,2]{2,1,0:T(1,128)}), s32[64,1,2]{2,1,0:T(1,128)S(1)}, u32[]{:S(2)}, u32[]{:S(2)}) async-start(s32[64,1,2]{2,1,0:T(1,128)} %copy.13), calls=%async_computation | async-start | bytes 65536 | tf_op jit(solution)/shard_map/all_to_all | solution.py:27
  21.9 8.5 %all-to-all-done = s32[64,1,2]{2,1,0:T(1,128)S(1)} async-done(((s32[64,1,2]{2,1,0:T(1,128)}), s32[64,1,2]{2,1,0:T(1,128)S(1)}, u32[]{:S(2)}, u32[]{:S(2)}) %all-to-all-start) | async-done | bytes 544 | tf_op jit(solution)/shard_map/all_to_all | solution.py:27
  30.8 6.6 gather_fusion
  37.4 5.9 all-to-all-start.1
  46.3 223.9 %collective-permute-done.1 = bf16[4096,256]{1,0:T(8,128)(2,1)} collective-permute-done((bf16[4096,256]{1,0:T(8,128)(2,1)}, bf16[4096,256]{1,0:T(8,128)(2,1)}, u32[]{:S(2)}, u32[]{:S(2)}) %collective-permute-start.1) | collective-permute-done | bytes 2097184 | tf_op jit(solution)/shard_map/ppermute | solution.py:10
  270.2 3.1 broadcast_select_fusion.2
  275.3 91.7 %collective-permute-done.2 = bf16[4096,256]{1,0:T(8,128)(2,1)} collective-permute-done((bf16[4096,256]{1,0:T(8,128)(2,1)}, bf16[4096,256]{1,0:T(8,128)(2,1)}, u32[]{:S(2)}, u32[]{:S(2)}) %collective-permute-start.2) | collective-permute-done | bytes 2097184 | tf_op jit(solution)/shard_map/ppermute | solution.py:10
  367.0 3.1 broadcast_select_fusion.3
  370.1 3.8 collective-permute-start.3
  373.8 92.5 %collective-permute-done.3 = bf16[4096,256]{1,0:T(8,128)(2,1)} collective-permute-done((bf16[4096,256]{1,0:T(8,128)(2,1)}, bf16[4096,256]{1,0:T(8,128)(2,1)}, u32[]{:S(2)}, u32[]{:S(2)}) %collective-permute-start.3) | collective-permute-done | bytes 2097184 | tf_op jit(solution)/shard_map/ppermute | solution.py:10
  466.4 3.1 broadcast_select_fusion.4
  470.4 45.3 %collective-permute-done.4 = bf16[4096,256]{1,0:T(8,128)(2,1)} collective-permute-done((bf16[4096,256]{1,0:T(8,128)(2,1)}, bf16[4096,256]{1,0:T(8,128)(2,1)}, u32[]{:S(2)}, u32[]{:S(2)}) %collective-permute-start.4) | collective-permute-done | bytes 2097184 | tf_op jit(solution)/shard_map/ppermute | solution.py:10
  515.7 3.1 broadcast_select_fusion.5
  518.9 3.1 collective-permute-start.5
  522.2 43.7 %collective-permute-done.5 = bf16[4096,256]{1,0:T(8,128)(2,1)} collective-permute-done((bf16[4096,256]{1,0:T(8,128)(2,1)}, bf16[4096,256]{1,0:T(8,128)(2,1)}, u32[]{:S(2)}, u32[]{:S(2)}) %collective-permute-start.5) | collective-permute-done | bytes 2097184 | tf_op jit(solution)/shard_map/ppermute | solution.py:10
  566.0 3.1 broadcast_select_fusion.6
  569.1 7.3 broadcast_select_fusion
  576.4 10.7 %pad_maximum_fusion = bf16[192,128,256]{2,1,0:T(8,128)(2,1)} fusion(bf16[128,128,256]{2,1,0:T(8,128)(2,1)} %bitcast.29, bf16[32,128,256]{2,1,0:T(8,128)(2,1)} %bitcast.33, bf16[32,128,256]{2,1,0:T(8,128)(2,1)S(1)} %bitcast.32), kind=kLoop, calls=%fused_computation.2 | loop fusion | flops 12582912 | bytes 25165824 | tf_op jit(solution)/shard_map/concatenate | solution.py:36
  587.0 14.4 %gather_fusion.1 = bf16[256,128,256]{2,1,0:T(8,128)(2,1)} fusion(bf16[192,128,256]{2,1,0:T(8,128)(2,1)} %pad_maximum_fusion, s32[1024]{0:T(1024)S(1)} %pad_clamp_fusion), kind=kCustom, calls=%fused_computation.1 | custom fusion | bytes 33555456 | tf_op jit(solution)/shard_map/gather | solution.py:44
  601.4 11.2 %bitcast_convert_fusion = bf16[32,256,128]{1,2,0:T(8,128)(2,1)S(1)} fusion(bf16[32,8,128,128]{3,2,1,0:T(8,128)(2,1)} %param.11, bf16[32,8,128,256]{3,2,1,0:T(8,128)(2,1)} %bitcast.28), kind=kOutput, calls=%fused_computation.4 | convolution fusion | flops 2148532224 | bytes 27262976 | tf_op jit(solution)/shard_map/tkij,tkjd->tid/dot_general | solution.py:45
  612.6 8.1 %fusion = f32[4096,1024]{1,0:T(8,128)} fusion(bf16[4096,256]{1,0:T(8,128)(2,1)S(1)} %bitcast.31, bf16[256,1024]{1,0:T(8,128)(2,1)S(1)} %copy-done.3), kind=kOutput, calls=%fused_computation.17 | convolution fusion | flops 2147483648 | bytes 19398656 | tf_op jit(solution)/shard_map/dot_general | solution.py:47
  620.7 152.5 %reduce-scatter.2.cloned.1.call-done = f32[4096,256]{1,0:T(8,128)} async-done(((f32[4096,1024]{1,0:T(8,128)}), f32[4096,256]{1,0:T(8,128)}) %reduce-scatter.2.cloned.1.call-update) | async-done | bytes 4194320 | tf_op jit(solution)/shard_map/reduce_scatter | solution.py:48
  773.2 3.9 maximum_convert_fusion
  (33 shorter events, 7.9 us)
Async XLA Ops:
  6.5 24.2 %copy-start = (bf16[2048,256]{1,0:T(8,128)(2,1)S(1)}, bf16[2048,256]{1,0:T(8,128)(2,1)}, u32[]{:S(2)}) copy-start(bf16[2048,256]{1,0:T(8,128)(2,1)} %param.10) | copy-start | bytes 3145732
  6.5 36.8 %collective-permute-start = (bf16[4096,256]{1,0:T(8,128)(2,1)}, bf16[4096,256]{1,0:T(8,128)(2,1)}, u32[]{:S(2)}, u32[]{:S(2)}) collective-permute-start(bf16[4096,256]{1,0:T(8,128)(2,1)} %param.9), channel_id=1, source_target_pairs={{0,4},{4,0},{8,12},{12,8},{16,20},{20,16},{24,28},{28,24},{32,36},... | collective-permute-start | bytes 6291464 | tf_op jit(solution)/shard_map/ppermute | solution.py:10
  11.2 19.3 %all-to-all-start = ((s32[64,1,2]{2,1,0:T(1,128)}), s32[64,1,2]{2,1,0:T(1,128)S(1)}, u32[]{:S(2)}, u32[]{:S(2)}) async-start(s32[64,1,2]{2,1,0:T(1,128)} %copy.13), calls=%async_computation | async-start | bytes 65536 | tf_op jit(solution)/shard_map/all_to_all | solution.py:27
  37.4 6.0 copy-start.2
  37.4 531.7 %all-to-all-start.1 = ((bf16[64,2,128,256]{3,2,1,0:T(8,128)(2,1)}), bf16[64,2,128,256]{3,2,1,0:T(8,128)(2,1)}, u32[]{:S(2)}, u32[]{:S(2)}) async-start(bf16[64,2,128,256]{3,2,1,0:T(8,128)(2,1)} %bitcast.30), calls=%async_computation.1 | async-start | bytes 16777216 | tf_op jit(solution)/shard_map/all_to_all | solution.py:26
  43.3 729.9 %reduce-scatter.2.cloned.1.call-start = ((), (), s32[]{:S(2)}) async-start(), calls=%async_computation.3 | async-start | bytes 20971520 | tf_op jit(solution)/shard_map/reduce_scatter | solution.py:48
  44.9 225.3 %collective-permute-start.1 = (bf16[4096,256]{1,0:T(8,128)(2,1)}, bf16[4096,256]{1,0:T(8,128)(2,1)}, u32[]{:S(2)}, u32[]{:S(2)}) collective-permute-start(bf16[4096,256]{1,0:T(8,128)(2,1)} %broadcast_select_fusion.1), channel_id=1, source_target_pairs={{0,8},{4,12},{8,0},{12,4},{16,24},{20,28},{24,16},{28,20},{32,40},... | collective-permute-start | bytes 6291464 | tf_op jit(solution)/shard_map/ppermute | solution.py:10
  273.3 93.6 %collective-permute-start.2 = (bf16[4096,256]{1,0:T(8,128)(2,1)}, bf16[4096,256]{1,0:T(8,128)(2,1)}, u32[]{:S(2)}, u32[]{:S(2)}) collective-permute-start(bf16[4096,256]{1,0:T(8,128)(2,1)} %broadcast_select_fusion.2), channel_id=1, source_target_pairs={{0,16},{4,20},{8,24},{12,28},{16,0},{20,4},{24,8},{28,12},{32,48},... | collective-permute-start | bytes 6291464 | tf_op jit(solution)/shard_map/ppermute | solution.py:10
  370.1 96.3 %collective-permute-start.3 = (bf16[4096,256]{1,0:T(8,128)(2,1)}, bf16[4096,256]{1,0:T(8,128)(2,1)}, u32[]{:S(2)}, u32[]{:S(2)}) collective-permute-start(bf16[4096,256]{1,0:T(8,128)(2,1)} %broadcast_select_fusion.3), channel_id=1, source_target_pairs={{0,32},{4,36},{8,40},{12,44},{16,48},{20,52},{24,56},{28,60},{32,0... | collective-permute-start | bytes 6291464 | tf_op jit(solution)/shard_map/ppermute | solution.py:10
  469.5 46.2 %collective-permute-start.4 = (bf16[4096,256]{1,0:T(8,128)(2,1)}, bf16[4096,256]{1,0:T(8,128)(2,1)}, u32[]{:S(2)}, u32[]{:S(2)}) collective-permute-start(bf16[4096,256]{1,0:T(8,128)(2,1)} %broadcast_select_fusion.4), channel_id=1, source_target_pairs={{0,64},{4,68},{8,72},{12,76},{16,80},{20,84},{24,88},{28,92},{32,9... | collective-permute-start | bytes 6291464 | tf_op jit(solution)/shard_map/ppermute | solution.py:10
  470.4 51.5 %copy-start.4 = (s32[32,8]{0,1:T(8,128)S(1)}, s32[32,8]{0,1:T(8,128)}, u32[]{:S(2)}) copy-start(s32[32,8]{0,1:T(8,128)} %param.12) | copy-start | bytes 3076
  470.4 51.7 %copy-start.6 = (s32[1,64]{1,0:T(1,128)S(1)}, s32[1,64]{1,0:T(1,128)}, u32[]{:S(2)}) copy-start(s32[1,64]{1,0:T(1,128)} %param.14) | copy-start | bytes 772
  518.9 47.1 %collective-permute-start.5 = (bf16[4096,256]{1,0:T(8,128)(2,1)}, bf16[4096,256]{1,0:T(8,128)(2,1)}, u32[]{:S(2)}, u32[]{:S(2)}) collective-permute-start(bf16[4096,256]{1,0:T(8,128)(2,1)} %broadcast_select_fusion.5), channel_id=1, source_target_pairs={{0,128},{4,132},{8,136},{12,140},{16,144},{20,148},{24,152},{28,15... | collective-permute-start | bytes 6291464 | tf_op jit(solution)/shard_map/ppermute | solution.py:10
  601.4 11.2 %copy-start.3 = (bf16[256,1024]{1,0:T(8,128)(2,1)S(1)}, bf16[256,1024]{1,0:T(8,128)(2,1)}, u32[]{:S(2)}) copy-start(bf16[256,1024]{1,0:T(8,128)(2,1)} %param.16) | copy-start | bytes 1572868
  620.7 152.5 %copy-start.5 = (f32[256]{0:T(256)S(1)}, f32[256]{0:T(256)}, u32[]{:S(2)}) copy-start(f32[256]{0:T(256)} %param.17) | copy-start | bytes 3076
  620.7 156.4 %copy-start.1 = (bf16[2048,256]{1,0:T(8,128)(2,1)S(1)}, bf16[2048,256]{1,0:T(8,128)(2,1)}, u32[]{:S(2)}) copy-start(bf16[2048,256]{1,0:T(8,128)(2,1)} %param.10) | copy-start | bytes 3145732
Sparse Core Ops, SparseCore 0:
  620.8 152.3 reduce-scatter.1
where the time goes:
time: 785 us; the launch traced here: 784 us
  waiting for transfers between devices  658 us (84%)
  other arithmetic  39.1 us (5%)
  starting transfers between devices  30.4 us (4%)
  local copies, waits for them, and re-layouts  22.8 us (3%)
  matrix products  19.3 us (2%)
  between operations  14.2 us (2%)
    ppermute x6, waiting for transfers between devices, from_partner(): return lax.ppermute(value, axis, pairs)  497 us
    reduce_scatter x1, waiting for transfers between devices, per_device(): mixed = lax.psum_scatter(term, 'mp', scatter_dimension=1, tiled=True)  152 us
    select_n x6, other arithmetic, per_device(): partner_rows = jnp.where(chosen, received, partner_rows)  17.2 us
  transfers between devices with their start and end apart: 9, of which 7 were waited for; matrix products, arithmetic and copies ran while one was open for 3% of the time, Pallas kernels for 0%

commit v1 on v0

v1 whole, which is shorter than its diff:
```python
import functools

import jax
import jax.numpy as jnp
from jax import lax
from jax.experimental import pallas as pl
from jax.experimental.pallas import tpu as pltpu
from jax.sharding import Mesh, PartitionSpec as P

NY, NZ, NC = 4, 8, 2
BLK = 128


def aggregate_kernel(src_idx, live, own, partner, pulled, adj, out, srcs, sems):
    t = pl.program_id(0)
    nb = own.shape[0]

    @pl.when(t == 0)
    def _():
        copies = [
            pltpu.make_async_copy(own, srcs.at[pl.ds(0, nb)], sems.at[0]),
            pltpu.make_async_copy(partner, srcs.at[pl.ds(nb, nb)], sems.at[1]),
            pltpu.make_async_copy(pulled, srcs.at[pl.ds(2 * nb, pulled.shape[0])], sems.at[2]),
        ]
        for copy in copies:
            copy.start()
        for copy in copies:
            copy.wait()

    kb = adj.shape[1]
    tiles, blocks = [], []
    for k in range(kb):
        tile = adj[0, k]
        tiles.append(jnp.where(live[t * kb + k] > 0, tile, jnp.zeros_like(tile)))
        blocks.append(srcs[src_idx[t * kb + k]])
    lhs = jnp.concatenate(tiles, axis=1)
    rhs = jnp.concatenate(blocks, axis=0)
    out[...] = jnp.dot(lhs, rhs, preferred_element_type=jnp.float32).astype(out.dtype)


def aggregate(src_idx, live, own, partner, pulled, adj):
    tb, kb = adj.shape[:2]
    width = own.shape[-1]
    n_src = own.shape[0] + partner.shape[0] + pulled.shape[0]
    return pl.pallas_call(
        aggregate_kernel,
        out_shape=jax.ShapeDtypeStruct((tb * BLK, width), jnp.bfloat16),
        grid_spec=pltpu.PrefetchScalarGridSpec(
            num_scalar_prefetch=2,
            grid=(tb,),
            in_specs=[
                pl.BlockSpec(memory_space=pl.ANY),
                pl.BlockSpec(memory_space=pl.ANY),
                pl.BlockSpec(memory_space=pl.ANY),
                pl.BlockSpec((1, kb, BLK, BLK), lambda t, *_: (t, 0, 0, 0)),
            ],
            out_specs=pl.BlockSpec((BLK, width), lambda t, *_: (t, 0)),
            scratch_shapes=[
                pltpu.VMEM((n_src, BLK, width), jnp.bfloat16),
                pltpu.SemaphoreType.DMA((3,)),
            ],
        ),
        compiler_params=pltpu.CompilerParams(vmem_limit_bytes=32 << 20),
        name="aggregate",
    )(src_idx, live, own, partner, pulled, adj)


def xor_permute(value, axes, size, which):
    def branch(m):
        if m == 0:
            return lambda v: v
        pairs = [(s, s ^ m) for s in range(size)]
        return lambda v: lax.ppermute(v, axes, pairs)

    return lax.switch(which, [branch(m) for m in range(size)], value)


def per_device(
    features, history, adj_values, adj_sources, pull_list, pull_count, partner_mask, weight, bias
):
    row_count, width = features.shape
    row_blocks = row_count // BLK
    cap = pull_list.shape[-1]
    hist_blocks = history.shape[0] // BLK
    mask = partner_mask[0]
    yc_mask = (mask >> 4) * NC + (mask & 1)
    z_mask = (mask >> 1) & (NZ - 1)

    hist_z = lax.all_gather(history, "z", axis=0, tiled=True)
    wanted = pull_list[0].reshape(NY, NZ, NC, cap).transpose(0, 2, 1, 3).reshape(NY * NC, NZ, cap)
    asked = lax.all_to_all(wanted, ("y", "core"), split_axis=0, concat_axis=0, tiled=True)
    block_ids = asked + jnp.arange(NZ, dtype=jnp.int32)[None, :, None] * hist_blocks

    half_way = xor_permute(features, ("y", "core"), NY * NC, yc_mask)
    hist_z, half_way, block_ids = lax.optimization_barrier((hist_z, half_way, block_ids))

    picked = hist_z.reshape(NZ * hist_blocks, BLK, width)[block_ids]
    pulled = lax.all_to_all(picked, ("y", "core"), split_axis=0, concat_axis=0, tiled=True)
    partner_rows = xor_permute(half_way, "z", NZ, z_mask)

    slot_no = jnp.maximum(adj_sources - 2 * row_blocks, 0)
    owner, slot = slot_no // cap, slot_no % cap
    oy, oz, oc = owner // (NZ * NC), (owner // NC) % NZ, owner % NC
    moved = ((oy * NC + oc) * NZ + oz) * cap + slot
    is_pulled = adj_sources >= 2 * row_blocks
    src_idx = jnp.where(is_pulled, 2 * row_blocks + moved, adj_sources)
    alive = (jnp.arange(cap)[None, :] < pull_count[0][:, None]).reshape(-1)
    live = jnp.where(is_pulled, alive[slot_no], True).astype(jnp.int32)

    agg = aggregate(
        src_idx.reshape(-1),
        live.reshape(-1),
        features.reshape(row_blocks, BLK, width),
        partner_rows.reshape(row_blocks, BLK, width),
        pulled.reshape(-1, BLK, width),
        adj_values,
    )
    w_cols = lax.all_to_all(weight, "mp", split_axis=1, concat_axis=0, tiled=True)
    agg_all = lax.all_gather(agg, "mp", axis=1, tiled=True)
    mixed = jnp.dot(agg_all, w_cols, preferred_element_type=jnp.float32)
    return jnp.maximum(mixed + bias, 0.0).astype(jnp.bfloat16)


def solution(mesh):
    n_mp = mesh.devices.shape[1]
    fine = Mesh(mesh.devices.reshape(NY, NZ, NC, n_mp), ("y", "z", "core", "mp"))
    dp = ("y", "z", "core")
    in_specs = (
        P(dp, "mp"),
        P(dp, "mp"),
        P(dp, None, None, None),
        P(dp, None),
        P(dp, None, None),
        P(dp, None),
        P(),
        P("mp", None),
        P("mp"),
    )
    return jax.shard_map(
        per_device, mesh=fine, in_specs=in_specs, out_specs=P(dp, "mp"), check_vma=False
    )
```

time: 785 us -> 340 us (0.43)
  waiting for transfers between devices: 658 us -> 253 us
  other arithmetic: 39.1 us -> 0.17 us
  Pallas kernels: 0 us -> 19 us
  starting transfers between devices: 30.4 us -> 14.8 us
  matrix products: 19.3 us -> 7.05 us
  blocking collectives: 0 us -> 12.1 us
    ppermute x6 -> x1, waiting for transfers between devices: 497 us -> 46.1 us  [branch(): return lambda v: lax.ppermute(v, axes, pairs)]
    reduce_scatter x1 -> x0, waiting for transfers between devices: 152 us -> none  [per_device(): mixed = lax.psum_scatter(term, 'mp', scatter_dimension=1, tiled=True)]
    all_gather x0 -> x2, waiting for transfers between devices: none -> 115 us  [the longest x1 72.3 us: per_device(): agg_all = lax.all_gather(agg, 'mp', axis=1, tiled=True)]
    all_to_all x2, waiting for transfers between devices: 8.55 us -> 91.2 us  [the longest x1 91.2 us: per_device(): lax.all_to_all(picked, ('y', 'core'), split_axis=0, concat_axis=0, tiled=...]
    select_n x9 -> x1, other arithmetic: 24.5 us -> 0.01 us  [per_device(): picked = hist_z.reshape(NZ * hist_blocks, BLK, width)[block_ids]]
    pallas_call x0 -> x1, Pallas kernels: none -> 19 us  [aggregate(): pl.pallas_call(aggregate_kernel, out_shape=jax.ShapeDtypeStruct((tb * BLK...]
    dot_general x2 -> x1, matrix products: 19.3 us -> 7.05 us  [per_device(): mixed = jnp.dot(agg_all, w_cols, preferred_element_type=jnp.float32)]
    all_to_all x0 -> x1, blocking collectives: none -> 12.1 us  [per_device(): lax.all_to_all(weight, 'mp', split_axis=1, concat_axis=0, tiled=True)]
  transfers between devices with their start and end apart: 9 -> 5, of which waited for: 7 -> 4; matrix products, arithmetic and copies ran while one was open for 3% -> 1% of each run, Pallas kernels for 0% -> 0%
where the time goes in v1:
time: 340 us; the launch traced here: 339 us
  waiting for transfers between devices  253 us (74%)
  local copies, waits for them, and re-layouts  19 us (6%)
  Pallas kernels  19 us (6%)
  starting transfers between devices  14.8 us (4%)
  between operations  14.2 us (4%)
  blocking collectives  12.1 us (4%)
  matrix products  7.05 us (2%)
    all_to_all x1, waiting for transfers between devices, per_device(): lax.all_to_all(picked, ('y', 'core'), split_axis=0, concat_axis=0, tiled=...  91.2 us
    all_gather x1, waiting for transfers between devices, per_device(): agg_all = lax.all_gather(agg, 'mp', axis=1, tiled=True)  72.3 us
    ppermute x1, waiting for transfers between devices, branch(): return lambda v: lax.ppermute(v, axes, pairs)  46.1 us
    all_gather x1, waiting for transfers between devices, per_device(): hist_z = lax.all_gather(history, 'z', axis=0, tiled=True)  42.3 us
    pallas_call x1, Pallas kernels, aggregate(): pl.pallas_call(aggregate_kernel, out_shape=jax.ShapeDtypeStruct((tb * BLK...  19 us
    all_to_all x1, blocking collectives, per_device(): lax.all_to_all(weight, 'mp', split_axis=1, concat_axis=0, tiled=True)  12.1 us
    gather x1, local copies, waits for them, and re-layouts, per_device(): picked = hist_z.reshape(NZ * hist_blocks, BLK, width)[block_ids]  9.94 us
    dot_general x1, matrix products, per_device(): mixed = jnp.dot(agg_all, w_cols, preferred_element_type=jnp.float32)  7.05 us
  transfers between devices with their start and end apart: 5, of which 4 were waited for; matrix products, arithmetic and copies ran while one was open for 1% of the time, Pallas kernels for 0%

profile of v1, /device:TPU:1, one launch (start us, length us, event | category | flops | bytes accessed | tf_op | source)
XLA Modules:
  0.0 339.1 jit_solution(4875088569531106789)
XLA Ops:
  6.5 0.7 all-gather.3.cloned.1.call-update
  7.3 0.8 reshape_squeeze.3
  8.0 0.1 copy.27
  8.2 0.6 copy.28
  8.8 6.5 %all-to-all-start = ((s32[8,8,2]{1,2,0:T(2,128)}), s32[8,8,2]{1,2,0:T(2,128)S(1)}, u32[]{:S(2)}, u32[]{:S(2)}) async-start(s32[8,8,2]{1,2,0:T(2,128)} %copy.28), calls=%async_computation | async-start | bytes 16384 | tf_op jit(solution)/shard_map/all_to_all | solution.py:91
  15.9 48.8 %conditional.2 = (bf16[4096,256]{1,0:T(8,128)(2,1)}) conditional(s32[]{:T(128)} %bitcast.11, bf16[4096,256]{1,0:T(8,128)(2,1)} %param.25, bf16[4096,256]{1,0:T(8,128)(2,1)} %param.25, bf16[4096,256]{1,0:T(8,128)(2,1)} %param.25, bf16[4096,256]{1,0:T(8,128)(2,1)} %param.25, bf16[4096,256]{1,0:T(8,128)(2,1)} %param.25, ...), branch_computations={%region_0.0_spmd, %region_1.0_spmd, %region_2.0_spmd, %region_3.0_... | conditional | bytes 8388656 | solution.py:75
  16.0 2.7 collective-permute-start.5
  18.7 46.1 %collective-permute-done.5 = bf16[4096,256]{1,0:T(8,128)(2,1)} collective-permute-done((bf16[4096,256]{1,0:T(8,128)(2,1)}, bf16[4096,256]{1,0:T(8,128)(2,1)}, u32[]{:S(2)}, u32[]{:S(2)}) %collective-permute-start.5) | collective-permute-done | bytes 2097184 | tf_op jit(solution)/shard_map/cond/branch_6_fun/ppermute | solution.py:73
  64.8 42.3 %all-gather.3.cloned.1.call-done = bf16[16384,256]{1,0:T(8,128)(2,1)} async-done(((bf16[2048,256]{1,0:T(8,128)(2,1)}), bf16[16384,256]{1,0:T(8,128)(2,1)}) %all-gather.3.cloned.1.call-update) | async-done | bytes 8388624 | tf_op jit(solution)/shard_map/all_gather | solution.py:89
  107.1 0.1 copy.29
  107.3 0.1 reshape.82
  107.4 9.9 %gather_fusion.1 = bf16[128,128,256]{2,1,0:T(8,128)(2,1)} fusion(bf16[128,128,256]{2,1,0:T(8,128)(2,1)} %bitcast.26, s32[1024]{0:T(1024)S(1)} %pad_clamp_fusion), kind=kCustom, calls=%fused_computation.1 | custom fusion | bytes 16777728 | tf_op jit(solution)/shard_map/gather | solution.py:97
  117.4 5.6 %all-to-all-start.1 = ((bf16[8,8,2,128,256]{4,3,2,1,0:T(8,128)(2,1)}), bf16[8,8,2,128,256]{4,3,2,1,0:T(8,128)(2,1)}, u32[]{:S(2)}, u32[]{:S(2)}) async-start(bf16[8,8,2,128,256]{4,3,2,1,0:T(8,128)(2,1)} %bitcast.24), calls=%async_computation.1 | async-start | bytes 16777216 | tf_op jit(solution)/shard_map/all_to_all | solution.py:98
  123.3 0.2 lt.47
  123.5 1.9 gather_fusion
  125.7 91.2 %all-to-all-done.1 = bf16[8,8,2,128,256]{4,3,2,1,0:T(8,128)(2,1)} async-done(((bf16[8,8,2,128,256]{4,3,2,1,0:T(8,128)(2,1)}), bf16[8,8,2,128,256]{4,3,2,1,0:T(8,128)(2,1)}, u32[]{:S(2)}, u32[]{:S(2)}) %all-to-all-start.1) | async-done | bytes 8388640 | tf_op jit(solution)/shard_map/all_to_all | solution.py:98
  216.9 3.4 copy-done
  220.3 19.0 %aggregate.1 = bf16[4096,256]{1,0:T(8,128)(2,1)} custom-call(s32[256]{0:T(256)S(1)} %reshape.54.src_idx, s32[256]{0:T(256)S(1)} %reshape.71.live, bf16[32,128,256]{2,1,0:T(8,128)(2,1)S(1)} %bitcast.25, bf16[32,128,256]{2,1,0:T(8,128)(2,1)} %get-tuple-element.51.partner, bf16[128,128,256]{2,1,0:T(8,128)(2,1)} %bitcast.16.pulled, ...), custom_call_target="tpu_custom_call" | custom-call | tf_op jit(solution)/shard_map/aggregate/pallas_call | solution.py:45
  239.3 1.0 copy-done.2
  240.3 0.2 copy.30
  240.5 12.1 %all_to_all.29 = bf16[256,4,256]{0,2,1:T(8,128)(2,1)S(1)} all-to-all(bf16[256,4,256]{0,2,1:T(8,128)(2,1)S(1)} %bitcast.35), channel_id=1, replica_groups=mesh['y'=4,'z'=8,'core'=2,'mp'=4] {'mp'}, dimensions={1} | all-to-all | bytes 1048576 | tf_op jit(solution)/shard_map/all_to_all | solution.py:118
  252.6 0.2 copy.31
  252.8 72.3 %all-gather.5.cloned.1.call-done = bf16[4096,1024]{1,0:T(8,128)(2,1)} async-done(((bf16[4096,256]{1,0:T(8,128)(2,1)}), bf16[4096,1024]{1,0:T(8,128)(2,1)}) %all-gather.5.cloned.1.call-update) | async-done | bytes 8388624 | tf_op jit(solution)/shard_map/all_gather | solution.py:119
  325.2 7.0 %fusion.1 = bf16[4096,256]{1,0:T(8,128)(2,1)} fusion(bf16[4096,1024]{1,0:T(8,128)(2,1)} %all-gather.5.cloned.1.call-done, bf16[1024,256]{1,0:T(8,128)(2,1)S(1)} %bitcast.36, f32[256]{0:T(256)S(1)} %copy-done.5), kind=kOutput, calls=%fused_computation.4 | convolution fusion | flops 2150629376 | bytes 11011072 | tf_op jit(solution)/shard_map/dot_general | solution.py:120
  (28 shorter events, 0.7 us)
Async XLA Ops:
  6.5 100.6 %all-gather.3.cloned.1.call-start = ((), (), s32[]{:S(2)}) async-start(), calls=%async_computation.3 | async-start | bytes 9437184 | tf_op jit(solution)/shard_map/all_gather | solution.py:89
  8.8 56.0 %all-to-all-start = ((s32[8,8,2]{1,2,0:T(2,128)}), s32[8,8,2]{1,2,0:T(2,128)S(1)}, u32[]{:S(2)}, u32[]{:S(2)}) async-start(s32[8,8,2]{1,2,0:T(2,128)} %copy.28), calls=%async_computation | async-start | bytes 16384 | tf_op jit(solution)/shard_map/all_to_all | solution.py:91
  16.0 48.8 %collective-permute-start.5 = (bf16[4096,256]{1,0:T(8,128)(2,1)}, bf16[4096,256]{1,0:T(8,128)(2,1)}, u32[]{:S(2)}, u32[]{:S(2)}) collective-permute-start(bf16[4096,256]{1,0:T(8,128)(2,1)} %param.6), channel_id=1, source_target_pairs={{0,192},{4,196},{64,128},{68,132},{128,64},{132,68},{192,0},{196,4... | collective-permute-start | bytes 6291464 | tf_op jit(solution)/shard_map/cond/branch_6_fun/ppermute | solution.py:73
  117.3 5.7 %copy-start.3 = (s32[32,8]{0,1:T(8,128)S(1)}, s32[32,8]{0,1:T(8,128)}, u32[]{:S(2)}) copy-start(s32[32,8]{0,1:T(8,128)} %param.28) | copy-start | bytes 3076
  117.4 5.9 %copy-start.4 = (s32[1,64]{1,0:T(1,128)S(1)}, s32[1,64]{1,0:T(1,128)}, u32[]{:S(2)}) copy-start(s32[1,64]{1,0:T(1,128)} %param.30) | copy-start | bytes 772
  117.4 99.5 %all-to-all-start.1 = ((bf16[8,8,2,128,256]{4,3,2,1,0:T(8,128)(2,1)}), bf16[8,8,2,128,256]{4,3,2,1,0:T(8,128)(2,1)}, u32[]{:S(2)}, u32[]{:S(2)}) async-start(bf16[8,8,2,128,256]{4,3,2,1,0:T(8,128)(2,1)} %bitcast.24), calls=%async_computation.1 | async-start | bytes 16777216 | tf_op jit(solution)/shard_map/all_to_all | solution.py:98
  123.0 202.2 %all-gather.5.cloned.1.call-start = ((), (), s32[]{:S(2)}) async-start(), calls=%async_computation.4 | async-start | bytes 10485760 | tf_op jit(solution)/shard_map/all_gather | solution.py:119
  125.7 91.2 %copy-start.1 = (bf16[4096,256]{1,0:T(8,128)(2,1)S(1)}, bf16[4096,256]{1,0:T(8,128)(2,1)}, u32[]{:S(2)}) copy-start(bf16[4096,256]{1,0:T(8,128)(2,1)} %param.25) | copy-start | bytes 6291460
  216.9 3.4 copy-start
  239.2 1.0 copy-start.2
  240.3 84.9 %copy-start.5 = (f32[256]{0:T(256)S(1)}, f32[256]{0:T(256)}, u32[]{:S(2)}) copy-start(f32[256]{0:T(256)} %param.33) | copy-start | bytes 3076
Sparse Core Ops, SparseCore 0:
  9.1 97.9 all-gather.2
  239.4 85.7 all-gather.4

commit v2 on v1

v2 whole, which is shorter than its diff:
```python
import jax
import jax.numpy as jnp
from jax import lax
from jax.experimental import pallas as pl
from jax.experimental.pallas import tpu as pltpu
from jax.sharding import Mesh, PartitionSpec as P

NY, NZ, NC = 4, 8, 2
BLK = 128
CHUNKS = 4
MESH = pl.DeviceIdType.MESH


def layer_kernel(
    n_mp, src_idx, own, partner, pulled, adj, wts, bias, out,
    srcs, tiles, agg_out, agg_in, res_out, load_sem, send_a, recv_a, send_b, recv_b,
):
    me = lax.axis_index("mp")
    tb, kb = adj.shape[:2]
    nb, n_pulled = own.shape[0], pulled.shape[0]
    n_src = 2 * nb + n_pulled
    per_dev = tb // n_mp
    per_chunk = per_dev // CHUNKS
    rows = per_chunk * BLK

    loads = [
        pltpu.make_async_copy(own, srcs.at[pl.ds(0, nb)], load_sem.at[0]),
        pltpu.make_async_copy(partner, srcs.at[pl.ds(nb, nb)], load_sem.at[1]),
        pltpu.make_async_copy(pulled, srcs.at[pl.ds(2 * nb, n_pulled)], load_sem.at[2]),
        pltpu.make_async_copy(adj, tiles, load_sem.at[3]),
    ]
    for load in loads:
        load.start()
    srcs[n_src] = jnp.zeros(srcs.shape[1:], srcs.dtype)

    barrier = pltpu.get_barrier_semaphore()
    for k in range(1, n_mp):
        pl.semaphore_signal(barrier, inc=1, device_id={"mp": (me + k) % n_mp}, device_id_type=MESH)
    pl.semaphore_wait(barrier, n_mp - 1)
    for load in loads:
        load.wait()

    def to_rows(q, k):
        return pltpu.make_async_remote_copy(
            src_ref=agg_out.at[q, k - 1],
            dst_ref=agg_in.at[q, k],
            send_sem=send_a.at[q, k - 1],
            recv_sem=recv_a.at[q, k - 1],
            device_id={"mp": (me + k) % n_mp},
            device_id_type=MESH,
        )

    def to_columns(q, k):
        return pltpu.make_async_remote_copy(
            src_ref=res_out.at[q, k - 1],
            dst_ref=out.at[pl.ds(pl.multiple_of((me * CHUNKS + q) * rows, rows), rows)],
            send_sem=send_b.at[q, k - 1],
            recv_sem=recv_b.at[q, k - 1],
            device_id={"mp": (me + k) % n_mp},
            device_id_type=MESH,
        )

    def aggregate(q, k, dst):
        first = ((me + k) % n_mp) * per_dev + q * per_chunk

        def one(i, carry):
            t = first + i
            lhs = jnp.concatenate([tiles[t, j] for j in range(kb)], axis=1)
            rhs = jnp.concatenate([srcs[src_idx[t * kb + j]] for j in range(kb)], axis=0)
            block = jnp.dot(lhs, rhs, preferred_element_type=jnp.float32)
            dst[pl.ds(pl.multiple_of(i * BLK, BLK), BLK), :] = block.astype(dst.dtype)
            return carry

        lax.fori_loop(0, per_chunk, one, 0)

    def multiply(q):
        for k in range(1, n_mp):
            to_rows(q, k).wait_recv()
        for n in list(range(1, n_mp)) + [0]:
            part = bias[(n_mp - n) % n_mp] + jnp.zeros((rows, 1), jnp.float32)
            for k in range(n_mp):
                part = part + jnp.dot(
                    agg_in[q, k], wts[k, (me + n) % n_mp], preferred_element_type=jnp.float32
                )
            part = jnp.maximum(part, 0.0).astype(out.dtype)
            if n:
                res_out[q, n - 1] = part
                to_columns(q, n).start()
            else:
                out[pl.ds(pl.multiple_of((me * CHUNKS + q) * rows, rows), rows), :] = part

    for q in range(CHUNKS + 1):
        if q < CHUNKS:
            for k in (2, 1, 3, 0):
                if k:
                    aggregate(q, k, agg_out.at[q, k - 1])
                    to_rows(q, k).start()
                else:
                    aggregate(q, k, agg_in.at[q, 0])
        if q:
            multiply(q - 1)
    for q in range(CHUNKS):
        for k in range(1, n_mp):
            to_rows(q, k).wait_send()
            to_columns(q, k).wait()


def layer(src_idx, own, partner, pulled, adj, wts, bias):
    n_mp = wts.shape[0]
    tb, kb = adj.shape[:2]
    width = own.shape[-1]
    n_src = own.shape[0] + partner.shape[0] + pulled.shape[0]
    rows = tb // n_mp // CHUNKS * BLK
    any_spec = pl.BlockSpec(memory_space=pl.ANY)
    vmem_spec = pl.BlockSpec(memory_space=pltpu.VMEM)

    def kernel(*refs):
        layer_kernel(n_mp, *refs)

    return pl.pallas_call(
        kernel,
        out_shape=jax.ShapeDtypeStruct((tb * BLK, width), jnp.bfloat16),
        in_specs=[pl.BlockSpec(memory_space=pltpu.SMEM)] + [any_spec] * 4 + [vmem_spec] * 2,
        out_specs=vmem_spec,
        scratch_shapes=[
            pltpu.VMEM((n_src + 1, BLK, width), jnp.bfloat16),
            pltpu.VMEM(adj.shape, jnp.bfloat16),
            pltpu.VMEM((CHUNKS, n_mp - 1, rows, width), jnp.bfloat16),
            pltpu.VMEM((CHUNKS, n_mp, rows, width), jnp.bfloat16),
            pltpu.VMEM((CHUNKS, n_mp - 1, rows, width), jnp.bfloat16),
            pltpu.SemaphoreType.DMA((4,)),
        ]
        + [pltpu.SemaphoreType.DMA((CHUNKS, n_mp - 1))] * 4,
        compiler_params=pltpu.CompilerParams(
            collective_id=0, has_side_effects=True, vmem_limit_bytes=44 << 20
        ),
        name="layer",
    )(src_idx, own, partner, pulled, adj, wts, bias)


def xor_permute(value, axes, size, which):
    def branch(m):
        if m == 0:
            return lambda v: v
        pairs = [(s, s ^ m) for s in range(size)]
        return lambda v: lax.ppermute(v, axes, pairs)

    return lax.switch(which, [branch(m) for m in range(size)], value)


def from_all(value, axis):
    n = lax.axis_size(axis)
    moved = [lax.ppermute(value, axis, [(s, (s + k) % n) for s in range(n)]) for k in range(1, n)]
    return jnp.stack([value] + moved)


def per_device(
    features, history, adj_values, adj_sources, pull_list, pull_count, partner_mask, weight, bias
):
    row_count, width = features.shape
    row_blocks = row_count // BLK
    cap = pull_list.shape[-1]
    hist_blocks = history.shape[0] // BLK
    mask = partner_mask[0]
    n_mp = lax.axis_size("mp")
    yc_mask = (mask >> 4) * NC + (mask & 1)
    z_mask = (mask >> 1) & (NZ - 1)

    hist_z = lax.all_gather(history, "z", axis=0, tiled=True)
    wanted = pull_list[0].reshape(NY, NZ, NC, cap).transpose(0, 2, 1, 3).reshape(NY * NC, NZ, cap)
    asked = lax.all_to_all(wanted, ("y", "core"), split_axis=0, concat_axis=0, tiled=True)
    block_ids = asked + jnp.arange(NZ, dtype=jnp.int32)[None, :, None] * hist_blocks

    wts = from_all(weight.reshape(width, n_mp, width).transpose(1, 0, 2), "mp")
    biases = from_all(bias.reshape(1, width), "mp")

    half_way = xor_permute(features, ("y", "core"), NY * NC, yc_mask)
    hist_z, half_way, block_ids, wts, biases = lax.optimization_barrier(
        (hist_z, half_way, block_ids, wts, biases)
    )

    picked = hist_z.reshape(NZ * hist_blocks, BLK, width)[block_ids]
    pulled = lax.all_to_all(picked, ("y", "core"), split_axis=0, concat_axis=0, tiled=True)
    partner_rows = xor_permute(half_way, "z", NZ, z_mask)

    slot_no = jnp.maximum(adj_sources - 2 * row_blocks, 0)
    owner, slot = slot_no // cap, slot_no % cap
    oy, oz, oc = owner // (NZ * NC), (owner // NC) % NZ, owner % NC
    moved = ((oy * NC + oc) * NZ + oz) * cap + slot
    alive = (jnp.arange(cap)[None, :] < pull_count[0][:, None]).reshape(-1)
    n_pulled = NY * NZ * NC * cap
    pulled_src = 2 * row_blocks + jnp.where(alive[slot_no], moved, n_pulled)
    src_idx = jnp.where(adj_sources >= 2 * row_blocks, pulled_src, adj_sources)

    return layer(
        src_idx.reshape(-1),
        features.reshape(row_blocks, BLK, width),
        partner_rows.reshape(row_blocks, BLK, width),
        pulled.reshape(-1, BLK, width),
        adj_values,
        wts,
        biases,
    )


def solution(mesh):
    n_mp = mesh.devices.shape[1]
    fine = Mesh(mesh.devices.reshape(NY, NZ, NC, n_mp), ("y", "z", "core", "mp"))
    dp = ("y", "z", "core")
    in_specs = (
        P(dp, "mp"),
        P(dp, "mp"),
        P(dp, None, None, None),
        P(dp, None),
        P(dp, None, None),
        P(dp, None),
        P(),
        P("mp", None),
        P("mp"),
    )
    return jax.shard_map(
        per_device, mesh=fine, in_specs=in_specs, out_specs=P(dp, "mp"), check_vma=False
    )
```

time: 340 us -> 286 us (0.84)
  waiting for transfers between devices: 253 us -> 172 us
  Pallas kernels: 19 us -> 56.9 us
  blocking collectives: 12.1 us -> 0 us
  starting transfers between devices: 14.8 us -> 23.3 us
  matrix products: 7.05 us -> 0 us
    ppermute x1 -> x2, waiting for transfers between devices: 46.1 us -> 139 us  [branch(): return lambda v: lax.ppermute(v, axes, pairs)]
    all_to_all x1, waiting for transfers between devices: 91.2 us -> 0.01 us  [per_device(): lax.all_to_all(picked, ('y', 'core'), split_axis=0, concat_axis=0, tiled=...]
    all_gather x1 -> x0, waiting for transfers between devices: 72.3 us -> none  [per_device(): agg_all = lax.all_gather(agg, 'mp', axis=1, tiled=True)]
    pallas_call x1, Pallas kernels: 19 us -> 56.9 us  [layer(): pl.pallas_call(kernel, out_shape=jax.ShapeDtypeStruct((tb * BLK, width),...]
    all_gather x1, waiting for transfers between devices: 42.3 us -> 27.7 us  [per_device(): hist_z = lax.all_gather(history, 'z', axis=0, tiled=True)]
    all_to_all x1 -> x0, blocking collectives: 12.1 us -> none  [per_device(): lax.all_to_all(weight, 'mp', split_axis=1, concat_axis=0, tiled=True)]
    ppermute x0 -> x6, starting transfers between devices: none -> 8.46 us  [from_all(): lax.ppermute(value, axis, [(s, (s + k) % n) for s in range(n)])]
    dot_general x1 -> x0, matrix products: 7.05 us -> none  [per_device(): mixed = jnp.dot(agg_all, w_cols, preferred_element_type=jnp.float32)]
  transfers between devices with their start and end apart: 5 -> 11, of which waited for: 4 -> 4; matrix products, arithmetic and copies ran while one was open for 1% -> 3% of each run, Pallas kernels for 0% -> 0%
where the time goes in v2:
time: 286 us
  waiting for transfers between devices  172 us (60%)
  Pallas kernels  56.9 us (20%)
  starting transfers between devices  23.3 us (8%)
  local copies, waits for them, and re-layouts  17.6 us (6%)
  between operations  14.2 us (5%)
    ppermute x2, waiting for transfers between devices, branch(): return lambda v: lax.ppermute(v, axes, pairs)  139 us
    pallas_call x1, Pallas kernels, layer(): pl.pallas_call(kernel, out_shape=jax.ShapeDtypeStruct((tb * BLK, width),...  56.9 us
    all_gather x1, waiting for transfers between devices, per_device(): hist_z = lax.all_gather(history, 'z', axis=0, tiled=True)  27.7 us
    gather x1, local copies, waits for them, and re-layouts, per_device(): picked = hist_z.reshape(NZ * hist_blocks, BLK, width)[block_ids]  9.96 us
    ppermute x6, starting transfers between devices, from_all(): lax.ppermute(value, axis, [(s, (s + k) % n) for s in range(n)])  8.46 us
  transfers between devices with their start and end apart: 11, of which 4 were waited for; matrix products, arithmetic and copies ran while one was open for 3% of the time, Pallas kernels for 0%

profile of v2, /device:TPU:1, one launch (start us, length us, event | category | flops | bytes accessed | tf_op | source)
XLA Modules:
  0.0 286.1 jit_solution(10170510121837334619)
XLA Ops:
  6.5 0.7 all-gather.2.cloned.1.call-update
  7.3 1.2 copy.24
  8.7 3.7 %collective-permute-start.15 = (bf16[4,256,256]{2,1,0:T(8,128)(2,1)S(1)}, bf16[4,256,256]{2,1,0:T(8,128)(2,1)S(1)}, u32[]{:S(2)}, u32[]{:S(2)}) collective-permute-start(bf16[4,256,256]{2,1,0:T(8,128)(2,1)S(1)} %bitcast.28), channel_id=1, source_target_pairs={{0,2},{1,3},{2,0},{3,1},{4,6},{5,7},{6,4},{7,5},{8,10},{9,11},{10,... | collective-permute-start | bytes 1572872 | tf_op jit(solution)/shard_map/ppermute | solution.py:153
  12.4 0.9 collective-permute-start.16
  13.2 0.6 collective-permute-start.14
  13.8 0.3 collective-permute-start.17
  14.8 49.6 %conditional.2 = (bf16[4096,256]{1,0:T(8,128)(2,1)}) conditional(s32[]{:T(128)} %bitcast.3, bf16[4096,256]{1,0:T(8,128)(2,1)S(1)} %copy-done, bf16[4096,256]{1,0:T(8,128)(2,1)S(1)} %copy-done, bf16[4096,256]{1,0:T(8,128)(2,1)S(1)} %copy-done, bf16[4096,256]{1,0:T(8,128)(2,1)S(1)} %copy-done, ...), branch_computations={%region_0.0_spmd, %region_1.0_spmd, %region_2.0_spmd, %region_3.0_... | conditional | bytes 8388656 | solution.py:148
  14.9 3.1 %collective-permute-start.2 = (bf16[4096,256]{1,0:T(8,128)(2,1)S(1)}, bf16[4096,256]{1,0:T(8,128)(2,1)}, u32[]{:S(2)}, u32[]{:S(2)}) collective-permute-start(bf16[4096,256]{1,0:T(8,128)(2,1)S(1)} %param.3), channel_id=1, source_target_pairs={{0,68},{4,64},{64,4},{68,0},{128,196},{132,192},{192,132},{196,128... | collective-permute-start | bytes 6291464 | tf_op jit(solution)/shard_map/cond/branch_3_fun/ppermute | solution.py:146
  17.9 46.5 %collective-permute-done.2 = bf16[4096,256]{1,0:T(8,128)(2,1)} collective-permute-done((bf16[4096,256]{1,0:T(8,128)(2,1)S(1)}, bf16[4096,256]{1,0:T(8,128)(2,1)}, u32[]{:S(2)}, u32[]{:S(2)}) %collective-permute-start.2) | collective-permute-done | bytes 2097184 | tf_op jit(solution)/shard_map/cond/branch_3_fun/ppermute | solution.py:146
  64.4 2.9 %collective-permute-start.18 = (f32[1,256]{1,0:T(1,128)S(1)}, f32[1,256]{1,0:T(1,128)S(1)}, u32[]{:S(2)}, u32[]{:S(2)}) collective-permute-start(f32[1,256]{1,0:T(1,128)S(1)} %bitcast.36), channel_id=1, source_target_pairs={{0,2},{1,3},{2,0},{3,1},{4,6},{5,7},{6,4},{7,5},{8,10},{9,11},{10,... | collective-permute-start | bytes 3080 | tf_op jit(solution)/shard_map/ppermute | solution.py:153
  67.6 0.6 copy.23
  68.2 5.0 %all-to-all-start = ((s32[8,8,2]{1,2,0:T(2,128)}), s32[8,8,2]{1,2,0:T(2,128)S(1)}, u32[]{:S(2)}, u32[]{:S(2)}) async-start(s32[8,8,2]{1,2,0:T(2,128)} %copy.23), calls=%async_computation | async-start | bytes 16384 | tf_op jit(solution)/shard_map/all_to_all | solution.py:171
  73.3 4.6 %all-to-all-done = s32[8,8,2]{1,2,0:T(2,128)S(1)} async-done(((s32[8,8,2]{1,2,0:T(2,128)}), s32[8,8,2]{1,2,0:T(2,128)S(1)}, u32[]{:S(2)}, u32[]{:S(2)}) %all-to-all-start) | async-done | bytes 544 | tf_op jit(solution)/shard_map/all_to_all | solution.py:171
  77.9 1.5 pad_maximum_fusion.refs_5_
  79.4 27.7 %all-gather.2.cloned.1.call-done = bf16[16384,256]{1,0:T(8,128)(2,1)} async-done(((bf16[2048,256]{1,0:T(8,128)(2,1)}), bf16[16384,256]{1,0:T(8,128)(2,1)}) %all-gather.2.cloned.1.call-update) | async-done | bytes 8388624 | tf_op jit(solution)/shard_map/all_gather | solution.py:169
  107.4 10.0 %gather_fusion.1 = bf16[128,128,256]{2,1,0:T(8,128)(2,1)} fusion(bf16[128,128,256]{2,1,0:T(8,128)(2,1)} %bitcast.25, s32[1024]{0:T(1024)S(1)} %pad_clamp_fusion), kind=kCustom, calls=%fused_computation.1 | custom fusion | bytes 16777728 | tf_op jit(solution)/shard_map/gather | solution.py:182
  117.4 5.6 %all-to-all-start.1 = ((bf16[8,8,2,128,256]{4,3,2,1,0:T(8,128)(2,1)}), bf16[8,8,2,128,256]{4,3,2,1,0:T(8,128)(2,1)}, u32[]{:S(2)}, u32[]{:S(2)}) async-start(bf16[8,8,2,128,256]{4,3,2,1,0:T(8,128)(2,1)} %bitcast.24), calls=%async_computation.1 | async-start | bytes 16777216 | tf_op jit(solution)/shard_map/all_to_all | solution.py:183
  123.4 1.9 gather_fusion
  125.5 95.5 %conditional.3 = (bf16[4096,256]{1,0:T(8,128)(2,1)}) conditional(s32[]{:T(128)} %bitcast.2, bf16[4096,256]{1,0:T(8,128)(2,1)} %get-tuple-element.65, bf16[4096,256]{1,0:T(8,128)(2,1)} %get-tuple-element.65, bf16[4096,256]{1,0:T(8,128)(2,1)} %get-tuple-element.65, bf16[4096,256]{1,0:T(8,128)(2,1)} %get-tuple-element.65, ...), branch_computations={%region_8.0_spmd, %region_9.0_spmd, %region_10.0_spmd, %region_11.... | conditional | bytes 12582960 | solution.py:148
  125.8 1.2 collective-permute-start.13
  127.0 92.7 %collective-permute-done.13 = bf16[4096,256]{1,0:T(8,128)(2,1)S(1)} collective-permute-done((bf16[4096,256]{1,0:T(8,128)(2,1)}, bf16[4096,256]{1,0:T(8,128)(2,1)S(1)}, u32[]{:S(2)}, u32[]{:S(2)}) %collective-permute-start.13) | collective-permute-done | bytes 2097184 | tf_op jit(solution)/shard_map/cond/branch_7_fun/ppermute | solution.py:146
  219.7 1.4 copy.42
  221.0 56.9 %layer.1 = bf16[4096,256]{1,0:T(8,128)(2,1)S(1)} custom-call(s32[256]{0:T(256)S(1)} %reshape.51.refs_0_, bf16[32,128,256]{2,1,0:T(8,128)(2,1)} %bitcast.26, bf16[32,128,256]{2,1,0:T(8,128)(2,1)} %bitcast.17.refs_2_, bf16[128,128,256]{2,1,0:T(8,128)(2,1)} %bitcast.20.refs_3_, bf16[32,8,128,128]{3,2,1,0:T(8,128)(2,1)} %refs_4_.1, ...), custom_call_target="tpu_custom_call" | custom-call | tf_op jit(solution)/shard_map/layer/pallas_call | solution.py:120
  277.9 1.3 copy.45
  (38 shorter events, 1.5 us)
Async XLA Ops:
  6.5 7.3 %copy-start.3 = (f32[256]{0:T(256)S(1)}, f32[256]{0:T(256)}, u32[]{:S(2)}) copy-start(f32[256]{0:T(256)} %param.33) | copy-start | bytes 3076
  6.5 8.3 %copy-start = (bf16[4096,256]{1,0:T(8,128)(2,1)S(1)}, bf16[4096,256]{1,0:T(8,128)(2,1)}, u32[]{:S(2)}) copy-start(bf16[4096,256]{1,0:T(8,128)(2,1)} %param.25) | copy-start | bytes 6291460
  6.5 100.6 %all-gather.2.cloned.1.call-start = ((), (), s32[]{:S(2)}) async-start(), calls=%async_computation.2 | async-start | bytes 9437184 | tf_op jit(solution)/shard_map/all_gather | solution.py:169
  8.7 69.2 %collective-permute-start.15 = (bf16[4,256,256]{2,1,0:T(8,128)(2,1)S(1)}, bf16[4,256,256]{2,1,0:T(8,128)(2,1)S(1)}, u32[]{:S(2)}, u32[]{:S(2)}) collective-permute-start(bf16[4,256,256]{2,1,0:T(8,128)(2,1)S(1)} %bitcast.28), channel_id=1, source_target_pairs={{0,2},{1,3},{2,0},{3,1},{4,6},{5,7},{6,4},{7,5},{8,10},{9,11},{10,... | collective-permute-start | bytes 1572872 | tf_op jit(solution)/shard_map/ppermute | solution.py:153
  12.4 65.5 %collective-permute-start.16 = (bf16[4,256,256]{2,1,0:T(8,128)(2,1)S(1)}, bf16[4,256,256]{2,1,0:T(8,128)(2,1)}, u32[]{:S(2)}, u32[]{:S(2)}) collective-permute-start(bf16[4,256,256]{2,1,0:T(8,128)(2,1)S(1)} %bitcast.29), channel_id=1, source_target_pairs={{0,3},{1,0},{2,1},{3,2},{4,7},{5,4},{6,5},{7,6},{8,11},{9,8},{10,9... | collective-permute-start | bytes 1572872 | tf_op jit(solution)/shard_map/ppermute | solution.py:153
  13.2 64.7 %collective-permute-start.14 = (bf16[4,256,256]{2,1,0:T(8,128)(2,1)S(1)}, bf16[4,256,256]{2,1,0:T(8,128)(2,1)}, u32[]{:S(2)}, u32[]{:S(2)}) collective-permute-start(bf16[4,256,256]{2,1,0:T(8,128)(2,1)S(1)} %bitcast.30), channel_id=1, source_target_pairs={{0,1},{1,2},{2,3},{3,0},{4,5},{5,6},{6,7},{7,4},{8,9},{9,10},{10,1... | collective-permute-start | bytes 1572872 | tf_op jit(solution)/shard_map/ppermute | solution.py:153
  13.8 59.3 %collective-permute-start.17 = (f32[1,256]{1,0:T(1,128)S(1)}, f32[1,256]{1,0:T(1,128)S(1)}, u32[]{:S(2)}, u32[]{:S(2)}) collective-permute-start(f32[1,256]{1,0:T(1,128)S(1)} %bitcast.35), channel_id=1, source_target_pairs={{0,1},{1,2},{2,3},{3,0},{4,5},{5,6},{6,7},{7,4},{8,9},{9,10},{10,1... | collective-permute-start | bytes 3080 | tf_op jit(solution)/shard_map/ppermute | solution.py:153
  14.8 52.5 %copy-start.2 = (s32[1,64,2]{1,2,0:T(2,128)S(1)}, s32[1,64,2]{1,2,0:T(2,128)}, u32[]{:S(2)}) copy-start(s32[1,64,2]{1,2,0:T(2,128)} %param.29) | copy-start | bytes 1540
  14.9 49.5 %collective-permute-start.2 = (bf16[4096,256]{1,0:T(8,128)(2,1)S(1)}, bf16[4096,256]{1,0:T(8,128)(2,1)}, u32[]{:S(2)}, u32[]{:S(2)}) collective-permute-start(bf16[4096,256]{1,0:T(8,128)(2,1)S(1)} %param.3), channel_id=1, source_target_pairs={{0,68},{4,64},{64,4},{68,0},{128,196},{132,192},{192,132},{196,128... | collective-permute-start | bytes 6291464 | tf_op jit(solution)/shard_map/cond/branch_3_fun/ppermute | solution.py:146
  64.4 13.5 %collective-permute-start.18 = (f32[1,256]{1,0:T(1,128)S(1)}, f32[1,256]{1,0:T(1,128)S(1)}, u32[]{:S(2)}, u32[]{:S(2)}) collective-permute-start(f32[1,256]{1,0:T(1,128)S(1)} %bitcast.36), channel_id=1, source_target_pairs={{0,2},{1,3},{2,0},{3,1},{4,6},{5,7},{6,4},{7,5},{8,10},{9,11},{10,... | collective-permute-start | bytes 3080 | tf_op jit(solution)/shard_map/ppermute | solution.py:153
  68.2 9.7 %all-to-all-start = ((s32[8,8,2]{1,2,0:T(2,128)}), s32[8,8,2]{1,2,0:T(2,128)S(1)}, u32[]{:S(2)}, u32[]{:S(2)}) async-start(s32[8,8,2]{1,2,0:T(2,128)} %copy.23), calls=%async_computation | async-start | bytes 16384 | tf_op jit(solution)/shard_map/all_to_all | solution.py:171
  73.2 4.7 %collective-permute-start.19 = (f32[1,256]{1,0:T(1,128)S(1)}, f32[1,256]{1,0:T(1,128)S(1)}, u32[]{:S(2)}, u32[]{:S(2)}) collective-permute-start(f32[1,256]{1,0:T(1,128)S(1)} %bitcast.37), channel_id=1, source_target_pairs={{0,3},{1,0},{2,1},{3,2},{4,7},{5,4},{6,5},{7,6},{8,11},{9,8},{10,9... | collective-permute-start | bytes 3080 | tf_op jit(solution)/shard_map/ppermute | solution.py:153
  117.4 5.6 %copy-start.1 = (s32[32,8]{0,1:T(8,128)S(1)}, s32[32,8]{0,1:T(8,128)}, u32[]{:S(2)}) copy-start(s32[32,8]{0,1:T(8,128)} %param.28) | copy-start | bytes 3076
  117.4 5.8 %copy-start.4 = (s32[1,64]{1,0:T(1,128)S(1)}, s32[1,64]{1,0:T(1,128)}, u32[]{:S(2)}) copy-start(s32[1,64]{1,0:T(1,128)} %param.30) | copy-start | bytes 772
  117.4 103.7 %all-to-all-start.1 = ((bf16[8,8,2,128,256]{4,3,2,1,0:T(8,128)(2,1)}), bf16[8,8,2,128,256]{4,3,2,1,0:T(8,128)(2,1)}, u32[]{:S(2)}, u32[]{:S(2)}) async-start(bf16[8,8,2,128,256]{4,3,2,1,0:T(8,128)(2,1)} %bitcast.24), calls=%async_computation.1 | async-start | bytes 16777216 | tf_op jit(solution)/shard_map/all_to_all | solution.py:183
  125.8 93.9 %collective-permute-start.13 = (bf16[4096,256]{1,0:T(8,128)(2,1)}, bf16[4096,256]{1,0:T(8,128)(2,1)S(1)}, u32[]{:S(2)}, u32[]{:S(2)}) collective-permute-start(bf16[4096,256]{1,0:T(8,128)(2,1)} %param.15), channel_id=1, source_target_pairs={{0,56},{8,48},{16,40},{24,32},{32,24},{40,16},{48,8},{56,0},{1,57}... | collective-permute-start | bytes 6291464 | tf_op jit(solution)/shard_map/cond/branch_7_fun/ppermute | solution.py:146
Sparse Core Ops, SparseCore 0:
  9.1 97.9 all-gather.1

commit v3 on v2

--- a/solution.py
+++ b/solution.py
@@ -138,6 +138,77 @@
     )(src_idx, own, partner, pulled, adj, wts, bias)
 
 
+def pull_kernel(block_ids, hist, out, held, picked, load_sem, send_sems, recv_sems):
+    y, core = lax.axis_index("y"), lax.axis_index("core")
+    me = y * NC + core
+    per_peer = picked.shape[1]
+
+    load = pltpu.make_async_copy(hist, held, load_sem.at[0])
+    load.start()
+    barrier = pltpu.get_barrier_semaphore()
+    peers = [(dy, dc) for dy in (2, 1, 3, 0) for dc in range(NC)]
+    peers.remove((0, 0))
+    for dy, dc in peers:
+        pl.semaphore_signal(
+            barrier, inc=1, device_id={"y": (y + dy) % NY, "core": (core + dc) % NC},
+            device_id_type=MESH,
+        )
+    pl.semaphore_wait(barrier, len(peers))
+    load.wait()
+
+    mine = out.at[pl.ds(me * per_peer, per_peer)]
+    copies = []
+    for n, (dy, dc) in enumerate(peers + [(0, 0)]):
+        to_y, to_core = (y + dy) % NY, (core + dc) % NC
+        first = (to_y * NC + to_core) * per_peer
+
+        def pick(s, carry):
+            picked[n, s] = held[block_ids[first + s]]
+            return carry
+
+        lax.fori_loop(0, per_peer, pick, 0)
+        if dy or dc:
+            copy = pltpu.make_async_remote_copy(
+                src_ref=picked.at[n],
+                dst_ref=mine,
+                send_sem=send_sems.at[n],
+                recv_sem=recv_sems.at[n],
+                device_id={"y": to_y, "core": to_core},
+                device_id_type=MESH,
+            )
+        else:
+            copy = pltpu.make_async_copy(picked.at[n], mine, load_sem.at[0])
+        copy.start()
+        copies.append(copy)
+    for copy in copies:
+        copy.wait()
+
+
+def pull(block_ids, hist):
+    n_peers = NY * NC
+    total = block_ids.shape[0]
+    width = hist.shape[-1]
+    any_spec = pl.BlockSpec(memory_space=pl.ANY)
+    return pl.pallas_call(
+        pull_kernel,
+        out_shape=jax.ShapeDtypeStruct((total, BLK, width), jnp.bfloat16),
+        in_specs=[pl.BlockSpec(memory_space=pltpu.SMEM), any_spec],
+        out_specs=any_spec,
+        scratch_shapes=[
+            pltpu.VMEM(hist.shape, jnp.bfloat16),
+            pltpu.VMEM((n_peers, total // n_peers, BLK, width), jnp.bfloat16),
+            pltpu.SemaphoreType.DMA((1,)),
+            pltpu.SemaphoreType.DMA((n_peers - 1,)),
+            pltpu.SemaphoreType.DMA((n_peers - 1,)),
+        ],
+        compiler_params=pltpu.CompilerParams(
+            collective_id=1, has_side_effects=True, vmem_limit_bytes=60 << 20
+        ),
+        cost_estimate=pl.CostEstimate(flops=0, bytes_accessed=256 << 20, transcendentals=0),
+        name="pull",
+    )(block_ids, hist)
+
+
 def xor_permute(value, axes, size, which):
     def branch(m):
         if m == 0:
@@ -179,9 +250,21 @@
         (hist_z, half_way, block_ids, wts, biases)
     )
 
-    picked = hist_z.reshape(NZ * hist_blocks, BLK, width)[block_ids]
-    pulled = lax.all_to_all(picked, ("y", "core"), split_axis=0, concat_axis=0, tiled=True)
-    partner_rows = xor_permute(half_way, "z", NZ, z_mask)
+    def pull_beside(m):
+        def branch(rows, ids, hist):
+            if m:
+                rows = lax.ppermute(rows, "z", [(s, s ^ m) for s in range(NZ)])
+            return rows, pull(ids, hist)
+
+        return branch
+
+    partner_rows, pulled = lax.switch(
+        z_mask,
+        [pull_beside(m) for m in range(NZ)],
+        half_way,
+        block_ids.reshape(-1),
+        hist_z.reshape(NZ * hist_blocks, BLK, width),
+    )
 
     slot_no = jnp.maximum(adj_sources - 2 * row_blocks, 0)
     owner, slot = slot_no // cap, slot_no % cap
@@ -196,7 +279,7 @@
         src_idx.reshape(-1),
         features.reshape(row_blocks, BLK, width),
         partner_rows.reshape(row_blocks, BLK, width),
-        pulled.reshape(-1, BLK, width),
+        pulled,
         adj_values,
         wts,
         biases,

time: 286 us -> 276 us (0.965)
  Pallas kernels: 56.9 us -> 155 us
  waiting for transfers between devices: 172 us -> 76.6 us
  local copies, waits for them, and re-layouts: 17.6 us -> 9.3 us
  starting transfers between devices: 23.3 us -> 18.8 us
    pallas_call x0 -> x1, Pallas kernels: none -> 98.1 us  [pull(): pl.pallas_call(pull_kernel, out_shape=jax.ShapeDtypeStruct((total, BLK, w...]
    ppermute x2 -> x1, waiting for transfers between devices: 139 us -> 46.2 us  [branch(): return lambda v: lax.ppermute(v, axes, pairs)]
    gather x1 -> x0, local copies, waits for them, and re-layouts: 9.96 us -> none  [per_device(): picked = hist_z.reshape(NZ * hist_blocks, BLK, width)[block_ids]]
    all_to_all x1 -> x0, starting transfers between devices: 5.61 us -> none  [per_device(): lax.all_to_all(picked, ('y', 'core'), split_axis=0, concat_axis=0, tiled=...]
  transfers between devices with their start and end apart: 11 -> 10, of which waited for: 4 -> 4; matrix products, arithmetic and copies ran while one was open for 3% -> 2% of each run, Pallas kernels for 0% -> 36%
where the time goes in v3:
time: 276 us
  Pallas kernels  155 us (56%)
  waiting for transfers between devices  76.6 us (28%)
  starting transfers between devices  18.8 us (7%)
  between operations  14.2 us (5%)
  local copies, waits for them, and re-layouts  9.3 us (3%)
    pallas_call x1, Pallas kernels, pull(): pl.pallas_call(pull_kernel, out_shape=jax.ShapeDtypeStruct((total, BLK, w...  98.1 us
    pallas_call x1, Pallas kernels, layer(): pl.pallas_call(kernel, out_shape=jax.ShapeDtypeStruct((tb * BLK, width),...  57.1 us
    ppermute x1, waiting for transfers between devices, branch(): return lambda v: lax.ppermute(v, axes, pairs)  46.2 us
    all_gather x1, waiting for transfers between devices, per_device(): hist_z = lax.all_gather(history, 'z', axis=0, tiled=True)  26.8 us
    ppermute x6, starting transfers between devices, from_all(): lax.ppermute(value, axis, [(s, (s + k) % n) for s in range(n)])  8.46 us
  transfers between devices with their start and end apart: 10, of which 4 were waited for; matrix products, arithmetic and copies ran while one was open for 2% of the time, Pallas kernels for 36%

profile of v3, /device:TPU:1, one launch (start us, length us, event | category | flops | bytes accessed | tf_op | source)
XLA Modules:
  0.0 276.0 jit_solution(10979799270251365288)
XLA Ops:
  6.5 0.7 all-gather.2.cloned.1.call-update
  7.3 1.2 copy.24
  8.5 0.2 copy.25
  8.7 3.7 %collective-permute-start.15 = (bf16[4,256,256]{2,1,0:T(8,128)(2,1)S(1)}, bf16[4,256,256]{2,1,0:T(8,128)(2,1)S(1)}, u32[]{:S(2)}, u32[]{:S(2)}) collective-permute-start(bf16[4,256,256]{2,1,0:T(8,128)(2,1)S(1)} %bitcast.32), channel_id=1, source_target_pairs={{0,2},{1,3},{2,0},{3,1},{4,6},{5,7},{6,4},{7,5},{8,10},{9,11},{10,... | collective-permute-start | bytes 1572872 | tf_op jit(solution)/shard_map/ppermute | solution.py:224
  12.4 0.9 collective-permute-start.16
  13.2 0.6 collective-permute-start.14
  13.8 0.3 collective-permute-start.17
  14.9 50.8 %conditional.2 = (bf16[4096,256]{1,0:T(8,128)(2,1)}) conditional(s32[]{:T(128)} %bitcast.3, bf16[4096,256]{1,0:T(8,128)(2,1)S(1)} %copy-done, bf16[4096,256]{1,0:T(8,128)(2,1)S(1)} %copy-done, bf16[4096,256]{1,0:T(8,128)(2,1)S(1)} %copy-done, bf16[4096,256]{1,0:T(8,128)(2,1)S(1)} %copy-done, ...), branch_computations={%region_0.0_spmd, %region_1.0_spmd, %region_2.0_spmd, %region_3.0_... | conditional | bytes 8388656 | solution.py:219
  14.9 4.5 %collective-permute-start.6 = (bf16[4096,256]{1,0:T(8,128)(2,1)S(1)}, bf16[4096,256]{1,0:T(8,128)(2,1)}, u32[]{:S(2)}, u32[]{:S(2)}) collective-permute-start(bf16[4096,256]{1,0:T(8,128)(2,1)S(1)} %param.7), channel_id=1, source_target_pairs={{0,196},{4,192},{64,132},{68,128},{128,68},{132,64},{192,4},{196,0... | collective-permute-start | bytes 6291464 | tf_op jit(solution)/shard_map/cond/branch_7_fun/ppermute | solution.py:217
  19.4 46.2 %collective-permute-done.6 = bf16[4096,256]{1,0:T(8,128)(2,1)} collective-permute-done((bf16[4096,256]{1,0:T(8,128)(2,1)S(1)}, bf16[4096,256]{1,0:T(8,128)(2,1)}, u32[]{:S(2)}, u32[]{:S(2)}) %collective-permute-start.6) | collective-permute-done | bytes 2097184 | tf_op jit(solution)/shard_map/cond/branch_7_fun/ppermute | solution.py:217
  65.6 2.9 %collective-permute-start.18 = (f32[1,256]{1,0:T(1,128)S(1)}, f32[1,256]{1,0:T(1,128)S(1)}, u32[]{:S(2)}, u32[]{:S(2)}) collective-permute-start(f32[1,256]{1,0:T(1,128)S(1)} %bitcast.40), channel_id=1, source_target_pairs={{0,2},{1,3},{2,0},{3,1},{4,6},{5,7},{6,4},{7,5},{8,10},{9,11},{10,... | collective-permute-start | bytes 3080 | tf_op jit(solution)/shard_map/ppermute | solution.py:224
  68.8 0.6 copy.23
  69.4 3.9 %all-to-all-start = ((s32[8,8,2]{1,2,0:T(2,128)}), s32[8,8,2]{1,2,0:T(2,128)S(1)}, u32[]{:S(2)}, u32[]{:S(2)}) async-start(s32[8,8,2]{1,2,0:T(2,128)} %copy.23), calls=%async_computation | async-start | bytes 16384 | tf_op jit(solution)/shard_map/all_to_all | solution.py:242
  73.7 1.9 gather_fusion
  76.0 2.0 all-to-all-done
  78.0 0.8 collective-permute-done.19
  78.8 1.5 pad_maximum_fusion.refs_5_
  80.3 26.8 %all-gather.2.cloned.1.call-done = bf16[16384,256]{1,0:T(8,128)(2,1)} async-done(((bf16[2048,256]{1,0:T(8,128)(2,1)}), bf16[16384,256]{1,0:T(8,128)(2,1)}) %all-gather.2.cloned.1.call-update) | async-done | bytes 8388624 | tf_op jit(solution)/shard_map/all_gather | solution.py:240
  107.4 103.4 %conditional.3 = (bf16[4096,256]{1,0:T(8,128)(2,1)}, bf16[128,128,256]{2,1,0:T(8,128)(2,1)}) conditional(s32[]{:T(128)} %bitcast.2, (s32[128]{0:T(128)S(1)}, bf16[128,128,256]{2,1,0:T(8,128)(2,1)}, bf16[4096,256]{1,0:T(8,128)(2,1)}) %tuple.83, (bf16[4096,256]{1,0:T(8,128)(2,1)}, s32[128]{0:T(128)S(1)}, ...), branch_computations={%region_8.0_spmd, %region_9.0_spmd, %region_10.0_spmd, %region_11.... | conditional | bytes 281018432 | solution.py:261
  107.6 2.0 collective-permute-start.12
  109.6 98.1 %pull.14 = bf16[128,128,256]{2,1,0:T(8,128)(2,1)} custom-call(s32[128]{0:T(128)S(1)} %get-tuple-element.89.block_ids, bf16[128,128,256]{2,1,0:T(8,128)(2,1)} %get-tuple-element.90.hist), custom_call_target="tpu_custom_call" | custom-call | bytes 268435456 | tf_op jit(solution)/shard_map/cond/branch_6_fun/pull/pallas_call | solution.py:192
  207.7 3.1 %copy.47 = bf16[4096,256]{1,0:T(8,128)(2,1)} copy(bf16[4096,256]{1,0:T(8,128)(2,1)} %collective-permute-done.12) | data formatting | bytes 4194304 | tf_op jit(solution)/shard_map/cond
  210.7 57.1 %layer.1 = bf16[4096,256]{1,0:T(8,128)(2,1)S(1)} custom-call(s32[256]{0:T(256)S(1)} %reshape.51.refs_0_, bf16[32,128,256]{2,1,0:T(8,128)(2,1)} %bitcast.30, bf16[32,128,256]{2,1,0:T(8,128)(2,1)} %bitcast.18.refs_2_, bf16[128,128,256]{2,1,0:T(8,128)(2,1)} %get-tuple-element.105.refs_3_, bf16[32,8,128,128]{3,2,1,0:T(8,128)(2,1)} %refs_4_.1, ...), custom_call_target="tpu_custom_call" | custom-call | tf_op jit(solution)/shard_map/layer/pallas_call | solution.py:120
  267.9 1.3 copy.53
  (34 shorter events, 1.3 us)
Async XLA Ops:
  6.5 7.3 %copy-start.3 = (f32[256]{0:T(256)S(1)}, f32[256]{0:T(256)}, u32[]{:S(2)}) copy-start(f32[256]{0:T(256)} %param.33) | copy-start | bytes 3076
  6.5 8.3 %copy-start = (bf16[4096,256]{1,0:T(8,128)(2,1)S(1)}, bf16[4096,256]{1,0:T(8,128)(2,1)}, u32[]{:S(2)}) copy-start(bf16[4096,256]{1,0:T(8,128)(2,1)} %param.25) | copy-start | bytes 6291460
  6.5 100.6 %all-gather.2.cloned.1.call-start = ((), (), s32[]{:S(2)}) async-start(), calls=%async_computation.1 | async-start | bytes 9437184 | tf_op jit(solution)/shard_map/all_gather | solution.py:240
  8.7 70.1 %collective-permute-start.15 = (bf16[4,256,256]{2,1,0:T(8,128)(2,1)S(1)}, bf16[4,256,256]{2,1,0:T(8,128)(2,1)S(1)}, u32[]{:S(2)}, u32[]{:S(2)}) collective-permute-start(bf16[4,256,256]{2,1,0:T(8,128)(2,1)S(1)} %bitcast.32), channel_id=1, source_target_pairs={{0,2},{1,3},{2,0},{3,1},{4,6},{5,7},{6,4},{7,5},{8,10},{9,11},{10,... | collective-permute-start | bytes 1572872 | tf_op jit(solution)/shard_map/ppermute | solution.py:224
  12.4 66.4 %collective-permute-start.16 = (bf16[4,256,256]{2,1,0:T(8,128)(2,1)S(1)}, bf16[4,256,256]{2,1,0:T(8,128)(2,1)}, u32[]{:S(2)}, u32[]{:S(2)}) collective-permute-start(bf16[4,256,256]{2,1,0:T(8,128)(2,1)S(1)} %bitcast.33), channel_id=1, source_target_pairs={{0,3},{1,0},{2,1},{3,2},{4,7},{5,4},{6,5},{7,6},{8,11},{9,8},{10,9... | collective-permute-start | bytes 1572872 | tf_op jit(solution)/shard_map/ppermute | solution.py:224
  13.2 65.6 %collective-permute-start.14 = (bf16[4,256,256]{2,1,0:T(8,128)(2,1)S(1)}, bf16[4,256,256]{2,1,0:T(8,128)(2,1)}, u32[]{:S(2)}, u32[]{:S(2)}) collective-permute-start(bf16[4,256,256]{2,1,0:T(8,128)(2,1)S(1)} %bitcast.34), channel_id=1, source_target_pairs={{0,1},{1,2},{2,3},{3,0},{4,5},{5,6},{6,7},{7,4},{8,9},{9,10},{10,1... | collective-permute-start | bytes 1572872 | tf_op jit(solution)/shard_map/ppermute | solution.py:224
  13.8 62.0 %collective-permute-start.17 = (f32[1,256]{1,0:T(1,128)S(1)}, f32[1,256]{1,0:T(1,128)S(1)}, u32[]{:S(2)}, u32[]{:S(2)}) collective-permute-start(f32[1,256]{1,0:T(1,128)S(1)} %bitcast.39), channel_id=1, source_target_pairs={{0,1},{1,2},{2,3},{3,0},{4,5},{5,6},{6,7},{7,4},{8,9},{9,10},{10,1... | collective-permute-start | bytes 3080 | tf_op jit(solution)/shard_map/ppermute | solution.py:224
  14.8 53.8 %copy-start.2 = (s32[1,64,2]{1,2,0:T(2,128)S(1)}, s32[1,64,2]{1,2,0:T(2,128)}, u32[]{:S(2)}) copy-start(s32[1,64,2]{1,2,0:T(2,128)} %param.29) | copy-start | bytes 1540
  14.8 58.4 %copy-start.1 = (s32[32,8]{0,1:T(8,128)S(1)}, s32[32,8]{0,1:T(8,128)}, u32[]{:S(2)}) copy-start(s32[32,8]{0,1:T(8,128)} %param.28) | copy-start | bytes 3076
  14.8 58.6 %copy-start.4 = (s32[1,64]{1,0:T(1,128)S(1)}, s32[1,64]{1,0:T(1,128)}, u32[]{:S(2)}) copy-start(s32[1,64]{1,0:T(1,128)} %param.30) | copy-start | bytes 772
  14.9 50.7 %collective-permute-start.6 = (bf16[4096,256]{1,0:T(8,128)(2,1)S(1)}, bf16[4096,256]{1,0:T(8,128)(2,1)}, u32[]{:S(2)}, u32[]{:S(2)}) collective-permute-start(bf16[4096,256]{1,0:T(8,128)(2,1)S(1)} %param.7), channel_id=1, source_target_pairs={{0,196},{4,192},{64,132},{68,128},{128,68},{132,64},{192,4},{196,0... | collective-permute-start | bytes 6291464 | tf_op jit(solution)/shard_map/cond/branch_7_fun/ppermute | solution.py:217
  65.6 12.3 %collective-permute-start.18 = (f32[1,256]{1,0:T(1,128)S(1)}, f32[1,256]{1,0:T(1,128)S(1)}, u32[]{:S(2)}, u32[]{:S(2)}) collective-permute-start(f32[1,256]{1,0:T(1,128)S(1)} %bitcast.40), channel_id=1, source_target_pairs={{0,2},{1,3},{2,0},{3,1},{4,6},{5,7},{6,4},{7,5},{8,10},{9,11},{10,... | collective-permute-start | bytes 3080 | tf_op jit(solution)/shard_map/ppermute | solution.py:224
  69.4 8.6 %all-to-all-start = ((s32[8,8,2]{1,2,0:T(2,128)}), s32[8,8,2]{1,2,0:T(2,128)S(1)}, u32[]{:S(2)}, u32[]{:S(2)}) async-start(s32[8,8,2]{1,2,0:T(2,128)} %copy.23), calls=%async_computation | async-start | bytes 16384 | tf_op jit(solution)/shard_map/all_to_all | solution.py:242
  75.9 2.9 %collective-permute-start.19 = (f32[1,256]{1,0:T(1,128)S(1)}, f32[1,256]{1,0:T(1,128)S(1)}, u32[]{:S(2)}, u32[]{:S(2)}) collective-permute-start(f32[1,256]{1,0:T(1,128)S(1)} %bitcast.41), channel_id=1, source_target_pairs={{0,3},{1,0},{2,1},{3,2},{4,7},{5,4},{6,5},{7,6},{8,11},{9,8},{10,9... | collective-permute-start | bytes 3080 | tf_op jit(solution)/shard_map/ppermute | solution.py:224
  107.6 100.1 %collective-permute-start.12 = (bf16[4096,256]{1,0:T(8,128)(2,1)}, bf16[4096,256]{1,0:T(8,128)(2,1)}, u32[]{:S(2)}, u32[]{:S(2)}) collective-permute-start(bf16[4096,256]{1,0:T(8,128)(2,1)} %get-tuple-element.88), channel_id=1, source_target_pairs={{0,48},{8,56},{16,32},{24,40},{32,16},{40,24},{48,0},{56,8},{1,49}... | collective-permute-start | bytes 6291464 | tf_op jit(solution)/shard_map/cond/branch_6_fun/ppermute | solution.py:256
Sparse Core Ops, SparseCore 0:
  9.1 97.9 all-gather.1
